TPU v7x, 32 devices: a whole 2x2x4 slice. The times are simulated.
32 devices in a mesh: groups: 2 (over y), blk: 4 (over z), col: 4 (over x, core).
Axes of the slice: x: 2, y: 2, z: 4, core: 2. Of those that a mesh axis runs over, the one named last changes fastest.
Arguments:
- aic: float32 [256, 32768], P(('groups', 'blk'), 'col'), parts along dimension 0, may hold values from -0.03125 to 0.03125
- downwash: float32 [8, 8192, 384], P(('groups', 'col'), 'blk'), parts along dimension 0, may hold values from -6 to 6
- node_modes: float32 [6, 32, 192], P(None, 'blk'), may hold values from -0.4375 to 0.4375
- src_rows: int32 [4, 4, 4, 8], P('blk', 'col'), may hold values from 0 to 7
- dst_nodes: int32 [4, 4, 4, 8], P('blk', 'col'), may hold values from 0 to 7
- counts: int32 [4, 4, 4], P('blk', 'col'), may hold values from 0 to 8, as said below
- spline_weights: float32 [4, 4, 6, 4, 8], P('blk', 'col'), may hold values from -0.6 to 0.6
Outputs:
- gaf: float32 [384, 384], P('groups'), parts along dimension 0
There are 2 independent parts, one for each index of `groups`. A program takes and returns all parts, laid end to end along the dimension named above; an argument that names none is the same for every part. Nothing has to cross between parts.
Inputs may be any that keep to these rules, and one draw needn't show every extreme that they name: `counts`: slot s of a list is live when s < count; every source sub-block sends 8 live slots to its own owner, and one owner receives 8 live slots from every source sub-block. `src_rows`: rows within a sub-block of 8 rows. `dst_nodes`: nodes within an owner.
All inputs are finite; a program needn't handle non-finite values.
Results may differ from a plain program's by a relative error of at most 0.0003.
Values sent between devices are 32-bit elements; how exact they have to be, the bound alone decides.
A program may use at most 64 MiB of HBM per device.

v0:
```python
import functools

import jax
import jax.numpy as jnp
from jax import lax
from jax.experimental import pallas as pl
from jax.experimental.pallas import tpu as pltpu
from jax.sharding import PartitionSpec as P


HIGHEST = lax.Precision.HIGHEST


def shifted(value, axis, steps):
    count = lax.axis_size(axis)
    pairs = [(source, (source + steps) % count) for source in range(count)]
    return lax.ppermute(value, axis, pairs)


def by_rotation(aic, downwash, node_modes, src_rows, dst_nodes, counts, spline_weights):
    cycle_size = lax.axis_size("blk")
    col_count = lax.axis_size("col")
    device = lax.axis_index("blk")
    own_block = downwash[0]
    panel_rows = own_block.shape[0]

    def product(shapes, source):
        columns = lax.dynamic_slice_in_dim(aic, source * panel_rows, panel_rows, 1)
        return jnp.dot(
            columns, shapes, precision=lax.Precision.HIGHEST, preferred_element_type=jnp.float32
        )

    halfway = cycle_size // 2

    def advance(offset, running):
        pressure, forward, behind = running
        forward = shifted(forward, "blk", 1)
        behind = shifted(behind, "blk", -1)
        pressure = pressure + product(forward, (device - offset) % cycle_size)
        pressure = pressure + product(behind, (device + offset) % cycle_size)
        return (pressure, forward, behind)

    pressure = product(own_block, device)
    pressure, forward, behind = lax.fori_loop(1, halfway, advance, (pressure, own_block, own_block))
    forward = shifted(forward, "blk", 1)
    pressure = pressure + product(forward, (device - halfway) % cycle_size)
    slots = src_rows.shape[-1]
    slot_index = jnp.arange(slots, dtype=jnp.int32)
    all_rows, all_nodes, all_counts = (
        lax.all_gather(src_rows, "col", axis=1, tiled=True),
        lax.all_gather(dst_nodes, "col", axis=1, tiled=True),
        lax.all_gather(counts, "col", axis=1, tiled=True),
    )
    weight_all = lax.all_gather(spline_weights, "col", axis=1, tiled=True)
    sub_rows = pressure.shape[0] // col_count
    offsets = jnp.arange(col_count, dtype=jnp.int32)[:, None, None] * sub_rows
    shifted_rows = all_rows[0] + offsets
    row_ids = jnp.transpose(shifted_rows, (1, 0, 2)).reshape(cycle_size, col_count * slots)
    node_ids = jnp.transpose(all_nodes[0], (1, 0, 2)).reshape(cycle_size, col_count * slots)
    live_sub = (slot_index[None, None, :] < all_counts[0][:, :, None]).astype(jnp.float32)
    live = jnp.transpose(live_sub, (1, 0, 2)).reshape(cycle_size, col_count * slots)
    weight_rows = jnp.transpose(weight_all[0], (1, 2, 0, 3)).reshape(
        6, cycle_size, col_count * slots
    )
    node_count = node_modes.shape[1]
    forces = pressure[row_ids.T]
    picks = (node_ids[None, :, :] == jnp.arange(node_count, dtype=jnp.int32)[:, None, None]).astype(
        jnp.float32
    )
    spread = weight_rows[:, None, :, :] * live[None, None, :, :] * picks[None, :, :, :]
    spread = spread.reshape(6 * node_count, cycle_size, row_ids.shape[1])
    arrived_forces, arrived_spread = (
        lax.all_to_all(forces, "blk", split_axis=1, concat_axis=1, tiled=True),
        lax.all_to_all(spread, "blk", split_axis=1, concat_axis=1, tiled=True),
    )
    loads = jnp.einsum(
        "jsc,csk->jk", arrived_spread, arrived_forces, precision=lax.Precision.HIGHEST
    )
    flat_modes = node_modes.reshape(6 * node_count, node_modes.shape[2])
    modal = jnp.einsum("jm,jk->mk", flat_modes, loads, precision=lax.Precision.HIGHEST)
    return lax.psum(modal, ("blk", "col"))


def split(value):
    high = value.astype(jnp.bfloat16)
    low = (value - high.astype(jnp.float32)).astype(jnp.bfloat16)
    return high, low


def exchange_kernel(
    blocks,
    cols,
    aic,
    panels,
    node_modes,
    rows_hbm,
    nodes_hbm,
    counts_hbm,
    weights_hbm,
    out,
    influence,
    shapes,
    shapes_high,
    shapes_low,
    partial,
    plane_in,
    line_in,
    pressure,
    spline,
    mode_rows,
    force,
    rows_list,
    nodes_list,
    counts,
    weights,
    list_sem,
    local_sem,
    aic_send,
    aic_recv,
    plane_send,
    plane_recv,
    line_send,
    line_recv,
    final_send,
    final_recv,
    spline_send,
    spline_recv,
    mode_send,
    mode_recv,
):
    b = lax.axis_index("blk")
    c = lax.axis_index("col")
    chunks, _, sub, depth = influence.shape
    dofs, _, node_count, modes = mode_rows.shape
    owners, slots = rows_list.shape[2:]
    width = panels.shape[2]
    senders = min(cols, dofs)
    while dofs % senders:
        senders -= 1
    share = dofs // senders
    pieces = local_sem.shape[0] - chunks - 1
    piece = depth // pieces

    def on_line(k):
        return lax.rem(b + k, blocks)

    def on_plane(k):
        return lax.rem(c + k, cols)

    def to_line(k, source, target, send, recv):
        return pltpu.make_async_remote_copy(
            src_ref=source,
            dst_ref=target,
            send_sem=send,
            recv_sem=recv,
            device_id={"blk": on_line(k)},
            device_id_type=pl.DeviceIdType.MESH,
        )

    def to_plane(k, source, target, send, recv):
        return pltpu.make_async_remote_copy(
            src_ref=source,
            dst_ref=target,
            send_sem=send,
            recv_sem=recv,
            device_id={"col": on_plane(k)},
            device_id_type=pl.DeviceIdType.MESH,
        )

    list_copies = []
    lists = ((rows_hbm, rows_list), (nodes_hbm, nodes_list), (counts_hbm, counts), (weights_hbm, weights))
    for i, (source, target) in enumerate(lists):
        list_copies.append(pltpu.make_async_copy(source, target, list_sem.at[i]))
        list_copies[-1].start()
    shape_copies = []
    for p in range(pieces):
        span = pl.ds(p * piece, piece)
        shape_copies.append(
            pltpu.make_async_copy(panels.at[0, span], shapes.at[span], local_sem.at[p])
        )
        shape_copies[-1].start()
    own_copies = []
    for q in range(chunks):
        own_copies.append(
            pltpu.make_async_copy(
                aic.at[pl.ds(q * sub, sub), pl.ds(pl.multiple_of(b * depth, depth), depth)],
                influence.at[q, b],
                local_sem.at[pieces + q],
            )
        )
        own_copies[-1].start()
    dof_span = pl.ds(lax.rem(c, senders) * share, share)
    own_modes = pltpu.make_async_copy(
        node_modes.at[dof_span], mode_rows.at[dof_span, b], local_sem.at[pieces + chunks]
    )

    barrier = pltpu.get_barrier_semaphore()
    for k in range(1, blocks):
        pl.semaphore_signal(
            barrier, inc=1, device_id={"blk": on_line(k)}, device_id_type=pl.DeviceIdType.MESH
        )
    for k in range(1, cols):
        pl.semaphore_signal(
            barrier, inc=1, device_id={"col": on_plane(k)}, device_id_type=pl.DeviceIdType.MESH
        )
    pl.semaphore_wait(barrier, blocks + cols - 2)

    aic_out = {}

    def send_rows(q):
        for k in range(1, blocks):
            peer = on_line(k)
            copy = to_line(
                k,
                aic.at[pl.ds(q * sub, sub), pl.ds(pl.multiple_of(peer * depth, depth), depth)],
                influence.at[q, b],
                aic_send.at[q, k - 1],
                aic_recv.at[q, k - 1],
            )
            copy.start()
            aic_out[q, k] = copy

    ahead = min(4, chunks)
    for q in range(ahead):
        send_rows(q)
        if q == 0:
            mode_out = [
                to_line(
                    k,
                    node_modes.at[dof_span],
                    mode_rows.at[dof_span, b],
                    mode_send.at[k - 1],
                    mode_recv.at[k - 1],
                )
                for k in range(1, blocks)
            ]

            @pl.when(c < senders)
            def _():
                own_modes.start()
                for copy in mode_out:
                    copy.start()

            length = dofs * owners * node_count
            row_at = lax.broadcasted_iota(jnp.int32, (sub, length), 0)
            column_at = lax.broadcasted_iota(jnp.int32, (sub, length), 1)
            total = jnp.zeros((sub, length), jnp.float32)
            for copy in list_copies:
                copy.wait()
            for o in range(owners):
                for s in range(slots):
                    live = s < counts[0, 0, o]
                    row = jnp.where(live, rows_list[0, 0, o, s], -1)
                    node = nodes_list[0, 0, o, s] + o * node_count
                    spread = jnp.zeros((sub, length), jnp.float32)
                    for d in range(dofs):
                        spread = jnp.where(
                            column_at == node + d * owners * node_count,
                            weights[0, 0, d, o, s],
                            spread,
                        )
                    total = total + jnp.where(row_at == row, spread, 0.0)
            spline[c, b] = total
            spline_out = []
            for k in range(1, blocks):
                copy = to_line(
                    k,
                    spline.at[c, b],
                    spline.at[c, b],
                    spline_send.at[k - 1],
                    spline_recv.at[k - 1],
                )
                copy.start()
                spline_out.append(copy)

    for p in range(pieces):
        shape_copies[p].wait()
        span = pl.ds(p * piece, piece)
        high, low = split(shapes[span])
        shapes_high[span] = high
        shapes_low[span] = low

    for copy in spline_out:
        copy.wait()
    for k in range(1, cols):
        copy = to_plane(
            k,
            spline.at[c],
            spline.at[c],
            spline_send.at[blocks - 2 + k],
            spline_recv.at[blocks - 2 + k],
        )
        copy.start()
        spline_out.append(copy)
    mode_plane = [
        to_plane(
            k,
            mode_rows.at[dof_span],
            mode_rows.at[dof_span],
            mode_send.at[blocks - 2 + k],
            mode_recv.at[blocks - 2 + k],
        )
        for k in range(1, cols)
    ]

    @pl.when(c < senders)
    def _():
        own_modes.wait()
        for copy in mode_out:
            copy.wait()
        for copy in mode_plane:
            copy.start()

    plane_out, line_out, final_out = {}, {}, {}

    def await_rows(q):
        own_copies[q].wait()
        for k in range(1, blocks):
            aic_out[q, k].wait_recv()

    def multiply(q):
        high, low = split(influence[q].reshape(blocks * sub, depth))
        product = jnp.dot(
            jnp.concatenate([high, low], axis=0),
            shapes_high[...],
            preferred_element_type=jnp.float32,
        )
        rest = jnp.dot(high, shapes_low[...], preferred_element_type=jnp.float32)
        lines = blocks * sub
        product = product[:lines] + (product[lines:] + rest)
        partial[q] = product.reshape(blocks, sub, width)
        for k in range(1, cols):
            copy = to_plane(
                k,
                partial.at[q, on_plane(k)],
                plane_in.at[q, k - 1],
                plane_send.at[q, k - 1],
                plane_recv.at[q, k - 1],
            )
            copy.start()
            plane_out[q, k] = copy

    def over_plane(q):
        total = partial[q, c]
        for k in range(1, cols):
            plane_out[q, k].wait_recv()
            total = total + plane_in[q, k - 1]
        line_in[q, b] = total
        for k in range(1, blocks):
            copy = to_line(
                k,
                line_in.at[q, b],
                line_in.at[q, b],
                line_send.at[q, k - 1],
                line_recv.at[q, k - 1],
            )
            copy.start()
            line_out[q, k] = copy

    def over_line(q):
        for k in range(1, blocks):
            line_out[q, k].wait_recv()
        total = line_in[q, 0]
        for source in range(1, blocks):
            total = total + line_in[q, source]
        pressure[q, c] = total
        for k in range(1, cols):
            copy = to_plane(
                k,
                pressure.at[q, c],
                pressure.at[q, c],
                final_send.at[q, k - 1],
                final_recv.at[q, k - 1],
            )
            copy.start()
            final_out[q, k] = copy

    def make_force():
        for k in range(1, cols):
            spline_out[blocks - 2 + k].wait_recv()

            @pl.when(lax.rem(c + cols - k, cols) < senders)
            def _():
                mode_plane[k - 1].wait_recv()

        length = dofs * owners * node_count
        force[...] = jnp.dot(
            spline[...].reshape(cols * blocks * sub, length),
            mode_rows[...].reshape(length, modes),
            precision=HIGHEST,
            preferred_element_type=jnp.float32,
        )

    def modal(start, stop):
        force_rows = force[pl.ds(start * blocks * sub, (stop - start) * blocks * sub)]
        return lax.dot_general(
            force_rows,
            pressure[start:stop].reshape((stop - start) * blocks * sub, width),
            (((0,), (0,)), ((), ())),
            precision=HIGHEST,
            preferred_element_type=jnp.float32,
        )

    def await_pressure(q):
        for k in range(1, cols):
            final_out[q, k].wait_recv()

    for q in range(chunks):
        await_rows(q)
        if q + ahead < chunks:
            send_rows(q + ahead)
        multiply(q)
        if q == chunks - 1:
            for earlier in range(q):
                over_plane(earlier)
        if q == 1:
            make_force()
    last = chunks - 1
    over_plane(last)
    for q in range(chunks):
        over_line(q)
    if last:
        for q in range(last):
            await_pressure(q)
        out[...] = modal(0, last)
        await_pressure(last)
        out[...] += modal(last, chunks)
    else:
        await_pressure(last)
        out[...] = modal(last, chunks)

    for copy in spline_out[blocks - 1 :]:
        copy.wait_send()
    for group in (aic_out, plane_out, line_out, final_out):
        for copy in group.values():
            copy.wait_send()

    @pl.when(c < senders)
    def _():
        for copy in mode_plane:
            copy.wait_send()


def by_kernel(aic, downwash, node_modes, src_rows, dst_nodes, counts, spline_weights):
    blocks = lax.axis_size("blk")
    cols = lax.axis_size("col")
    rows = aic.shape[0]
    sub = rows // cols
    depth, width = downwash.shape[1:]
    dofs, node_count, modes = node_modes.shape
    length = dofs * blocks * node_count
    pieces = 4
    dma = pltpu.SemaphoreType.DMA
    anywhere = pl.BlockSpec(memory_space=pl.ANY)
    return pl.pallas_call(
        functools.partial(exchange_kernel, blocks, cols),
        name="gaf_exchange",
        out_shape=jax.ShapeDtypeStruct((modes, width), jnp.float32),
        in_specs=[anywhere] * 7,
        out_specs=pl.BlockSpec(memory_space=pltpu.VMEM),
        scratch_shapes=[
            pltpu.VMEM((cols, blocks, sub, depth), jnp.float32),
            pltpu.VMEM((depth, width), jnp.float32),
            pltpu.VMEM((depth, width), jnp.bfloat16),
            pltpu.VMEM((depth, width), jnp.bfloat16),
            pltpu.VMEM((cols, blocks, sub, width), jnp.float32),
            pltpu.VMEM((cols, cols - 1, sub, width), jnp.float32),
            pltpu.VMEM((cols, blocks, sub, width), jnp.float32),
            pltpu.VMEM((cols, blocks, sub, width), jnp.float32),
            pltpu.VMEM((cols, blocks, sub, length), jnp.float32),
            pltpu.VMEM((dofs, blocks, node_count, modes), jnp.float32),
            pltpu.VMEM((cols * blocks * sub, modes), jnp.float32),
            pltpu.SMEM(src_rows.shape, jnp.int32),
            pltpu.SMEM(dst_nodes.shape, jnp.int32),
            pltpu.SMEM(counts.shape, jnp.int32),
            pltpu.SMEM(spline_weights.shape, jnp.float32),
            dma((4,)),
            dma((pieces + cols + 1,)),
            dma((cols, blocks - 1)),
            dma((cols, blocks - 1)),
            dma((cols, cols - 1)),
            dma((cols, cols - 1)),
            dma((cols, blocks - 1)),
            dma((cols, blocks - 1)),
            dma((cols, cols - 1)),
            dma((cols, cols - 1)),
            dma((blocks + cols - 2,)),
            dma((blocks + cols - 2,)),
            dma((blocks + cols - 2,)),
            dma((blocks + cols - 2,)),
        ],
        compiler_params=pltpu.CompilerParams(
            collective_id=0, has_side_effects=True, vmem_limit_bytes=60 * 1024 * 1024
        ),
    )(aic, downwash, node_modes, src_rows, dst_nodes, counts, spline_weights)


def solution(mesh):
    placed = (
        P(("groups", "blk"), "col"),
        P(("groups", "col"), "blk", None),
        P(None, "blk", None),
        P("blk", "col", None, None),
        P("blk", "col", None, None),
        P("blk", "col", None),
        P("blk", "col", None, None, None),
    )

    def shards(*operands):
        aic, downwash, node_modes = operands[:3]
        blocks, cols = lax.axis_size("blk"), lax.axis_size("col")
        small = blocks * aic.shape[0] <= 2 * node_modes.shape[2]
        even = blocks == cols and aic.shape[0] % (8 * cols) == 0 and downwash.shape[1] % 512 == 0
        if small and even:
            return by_kernel(*operands)
        return by_rotation(*operands)

    return jax.shard_map(
        shards, mesh=mesh, in_specs=placed, out_specs=P("groups", None), check_vma=False
    )
```

profile of v0, /device:TPU:0, one launch (start us, length us, event | category | flops | bytes accessed | tf_op | source)
XLA Modules:
  0.0 45.3 jit_solution(2808780791326669564)
XLA Ops:
  0.0 43.6 %gaf_exchange.1 = f32[192,384]{1,0:T(8,128)} custom-call(f32[32,8192]{1,0:T(8,128)} %aic.1, f32[1,2048,384]{2,1,0:T(8,128)} %panels.1, f32[6,8,192]{2,1,0:T(8,128)} %node_modes.1, s32[1,1,4,8]{3,2,1,0:T(4,128)} %rows_hbm.1, s32[1,1,4,8]{3,2,1,0:T(4,128)} %nodes_hbm.1, s32[1,1,4]{2,1,0:T(1,128)} %counts_hbm.1, f32[1,1,6,4,8]{4,3,2,1,0:T(4,128)} %weights_hbm.1), custom_call_target="tpu_custom_call" | custom-call | tf_op jit(solution)/shard_map/gaf_exchange/pallas_call | solution.py:455
  43.6 1.7 %copy.9 = f32[192,384]{1,0:T(8,128)} copy(f32[192,384]{1,0:T(8,128)} %gaf_exchange.1) | data formatting | bytes 589824
where the time goes:
time: 45.4 us; the launch traced here: 45.3 us
  Pallas kernels  43.6 us (96%)
  local copies, waits for them, and re-layouts  1.69 us (4%)
    pallas_call x1, Pallas kernels, by_kernel(): pl.pallas_call(functools.partial(exchange_kernel, blocks, cols), name='ga...  43.6 us
    unnamed x1, local copies, waits for them, and re-layouts  1.69 us

commit v1 on v0

--- a/solution.py
+++ b/solution.py
@@ -452,6 +452,8 @@
     pieces = 4
     dma = pltpu.SemaphoreType.DMA
     anywhere = pl.BlockSpec(memory_space=pl.ANY)
+    operands = (aic, downwash, node_modes, src_rows, dst_nodes, counts, spline_weights)
+    in_hbm = [pltpu.with_memory_space_constraint(v, pltpu.MemorySpace.HBM) for v in operands]
     return pl.pallas_call(
         functools.partial(exchange_kernel, blocks, cols),
         name="gaf_exchange",
@@ -490,9 +492,9 @@
             dma((blocks + cols - 2,)),
         ],
         compiler_params=pltpu.CompilerParams(
-            collective_id=0, has_side_effects=True, vmem_limit_bytes=60 * 1024 * 1024
+            collective_id=0, has_side_effects=True, vmem_limit_bytes=32 * 1024 * 1024
         ),
-    )(aic, downwash, node_modes, src_rows, dst_nodes, counts, spline_weights)
+    )(*in_hbm)
 
 
 def solution(mesh):

time: 45.4 us -> 43.7 us (0.963)
  local copies, waits for them, and re-layouts: 1.69 us -> 0.72 us
  Pallas kernels: 43.6 us -> 42.8 us
    unnamed x1, local copies, waits for them, and re-layouts: 1.69 us -> 0.72 us
    pallas_call x1, Pallas kernels: 43.6 us -> 42.8 us  [by_kernel(): pl.pallas_call(functools.partial(exchange_kernel, blocks, cols), name='ga...]
where the time goes in v1:
time: 43.7 us; the launch traced here: 43.6 us
  Pallas kernels  42.8 us (98%)
  local copies, waits for them, and re-layouts  0.72 us (2%)
    pallas_call x1, Pallas kernels, by_kernel(): pl.pallas_call(functools.partial(exchange_kernel, blocks, cols), name='ga...  42.8 us

profile of v1, /device:TPU:0, one launch (start us, length us, event | category | flops | bytes accessed | tf_op | source)
XLA Modules:
  0.0 43.6 jit_solution(14840996436963174588)
XLA Ops:
  0.0 42.8 %gaf_exchange.1 = f32[192,384]{1,0:T(8,128)S(1)} custom-call(f32[32,8192]{1,0:T(8,128)} %aic.1, f32[1,2048,384]{2,1,0:T(8,128)} %panels.1, f32[6,8,192]{2,1,0:T(8,128)} %node_modes.1, s32[1,1,4,8]{3,2,1,0:T(4,128)} %rows_hbm.1, s32[1,1,4,8]{3,2,1,0:T(4,128)} %nodes_hbm.1, s32[1,1,4]{2,1,0:T(1,128)} %counts_hbm.1, f32[1,1,6,4,8]{4,3,2,1,0:T(4,128)} %weights_hbm.1), custom_call_target="tpu_custom_call" | custom-call | tf_op jit(solution)/shard_map/gaf_exchange/pallas_call | solution.py:457
  42.9 0.7 %copy.9 = f32[192,384]{1,0:T(8,128)} copy(f32[192,384]{1,0:T(8,128)S(1)} %gaf_exchange.1) | data formatting | bytes 589824

commit v2 on v1

v2 whole, which is shorter than its diff:
```python
import functools

import jax
import jax.numpy as jnp
from jax import lax
from jax.experimental import pallas as pl
from jax.experimental.pallas import tpu as pltpu
from jax.sharding import PartitionSpec as P


HIGHEST = lax.Precision.HIGHEST
PARTS = 2
AHEAD = 4
OWNED = (0,)
LISTS_AT = 3
SPREAD_AT = 7
ODD_AHEAD = 2


def shifted(value, axis, steps):
    count = lax.axis_size(axis)
    pairs = [(source, (source + steps) % count) for source in range(count)]
    return lax.ppermute(value, axis, pairs)


def by_rotation(aic, downwash, node_modes, src_rows, dst_nodes, counts, spline_weights):
    cycle_size = lax.axis_size("blk")
    col_count = lax.axis_size("col")
    device = lax.axis_index("blk")
    own_block = downwash[0]
    panel_rows = own_block.shape[0]

    def product(shapes, source):
        columns = lax.dynamic_slice_in_dim(aic, source * panel_rows, panel_rows, 1)
        return jnp.dot(
            columns, shapes, precision=lax.Precision.HIGHEST, preferred_element_type=jnp.float32
        )

    halfway = cycle_size // 2

    def advance(offset, running):
        pressure, forward, behind = running
        forward = shifted(forward, "blk", 1)
        behind = shifted(behind, "blk", -1)
        pressure = pressure + product(forward, (device - offset) % cycle_size)
        pressure = pressure + product(behind, (device + offset) % cycle_size)
        return (pressure, forward, behind)

    pressure = product(own_block, device)
    pressure, forward, behind = lax.fori_loop(1, halfway, advance, (pressure, own_block, own_block))
    forward = shifted(forward, "blk", 1)
    pressure = pressure + product(forward, (device - halfway) % cycle_size)
    slots = src_rows.shape[-1]
    slot_index = jnp.arange(slots, dtype=jnp.int32)
    all_rows, all_nodes, all_counts = (
        lax.all_gather(src_rows, "col", axis=1, tiled=True),
        lax.all_gather(dst_nodes, "col", axis=1, tiled=True),
        lax.all_gather(counts, "col", axis=1, tiled=True),
    )
    weight_all = lax.all_gather(spline_weights, "col", axis=1, tiled=True)
    sub_rows = pressure.shape[0] // col_count
    offsets = jnp.arange(col_count, dtype=jnp.int32)[:, None, None] * sub_rows
    shifted_rows = all_rows[0] + offsets
    row_ids = jnp.transpose(shifted_rows, (1, 0, 2)).reshape(cycle_size, col_count * slots)
    node_ids = jnp.transpose(all_nodes[0], (1, 0, 2)).reshape(cycle_size, col_count * slots)
    live_sub = (slot_index[None, None, :] < all_counts[0][:, :, None]).astype(jnp.float32)
    live = jnp.transpose(live_sub, (1, 0, 2)).reshape(cycle_size, col_count * slots)
    weight_rows = jnp.transpose(weight_all[0], (1, 2, 0, 3)).reshape(
        6, cycle_size, col_count * slots
    )
    node_count = node_modes.shape[1]
    forces = pressure[row_ids.T]
    picks = (node_ids[None, :, :] == jnp.arange(node_count, dtype=jnp.int32)[:, None, None]).astype(
        jnp.float32
    )
    spread = weight_rows[:, None, :, :] * live[None, None, :, :] * picks[None, :, :, :]
    spread = spread.reshape(6 * node_count, cycle_size, row_ids.shape[1])
    arrived_forces, arrived_spread = (
        lax.all_to_all(forces, "blk", split_axis=1, concat_axis=1, tiled=True),
        lax.all_to_all(spread, "blk", split_axis=1, concat_axis=1, tiled=True),
    )
    loads = jnp.einsum(
        "jsc,csk->jk", arrived_spread, arrived_forces, precision=lax.Precision.HIGHEST
    )
    flat_modes = node_modes.reshape(6 * node_count, node_modes.shape[2])
    modal = jnp.einsum("jm,jk->mk", flat_modes, loads, precision=lax.Precision.HIGHEST)
    return lax.psum(modal, ("blk", "col"))


def split(value):
    high = value.astype(jnp.bfloat16)
    low = (value - high.astype(jnp.float32)).astype(jnp.bfloat16)
    return high, low


def exchange_kernel(
    blocks,
    cols,
    aic,
    panels,
    node_modes,
    rows_hbm,
    nodes_hbm,
    counts_hbm,
    weights_hbm,
    out,
    influence,
    shapes,
    shapes_high,
    shapes_low,
    partial,
    plane_in,
    line_in,
    gather_in,
    pressure,
    spline,
    mode_rows,
    force,
    rows_list,
    nodes_list,
    counts,
    weights,
    list_sem,
    panel_sem,
    aic_recv,
    aic_send,
    plane_recv,
    plane_send,
    line_recv,
    line_send,
    back_recv,
    final_recv,
    final_send,
    gather_recv,
    gather_send,
    cast_recv,
    cast_send,
    spline_recv,
    spline_send,
    mode_recv,
    mode_send,
    mode_plane_recv,
):
    b = lax.axis_index("blk")
    c = lax.axis_index("col")
    chunks, _, sub, depth = influence.shape
    dofs, _, node_count, modes = mode_rows.shape
    owners, slots = rows_list.shape[2:]
    width = panels.shape[2]
    last = chunks - 1
    early = range(last)
    parts = PARTS
    span = depth // parts
    total_pieces = chunks * parts
    middle = blocks // 2
    length = dofs * owners * node_count

    def on_line(k):
        return lax.rem(b + k, blocks)

    def on_plane(k):
        return lax.rem(c + k, cols)

    def far_target(j):
        falling = blocks - 1 - j
        rising = j
        falling = jnp.where(falling <= b, falling - 1, falling)
        rising = jnp.where(rising >= b, rising + 1, rising)
        return jnp.where(b < middle, falling, rising)

    def remote(where, source, target, send, recv):
        return pltpu.make_async_remote_copy(
            src_ref=source,
            dst_ref=target,
            send_sem=send,
            recv_sem=recv,
            device_id=where,
            device_id_type=pl.DeviceIdType.MESH,
        )

    def settle(ref, sem):
        pltpu.make_async_copy(ref, ref, sem).wait()

    barrier = pltpu.get_barrier_semaphore()
    for z in range(blocks):
        for x in range(cols):
            if (z == 0) != (x == 0):
                pl.semaphore_signal(
                    barrier,
                    inc=1,
                    device_id={"blk": on_line(z), "col": on_plane(x)},
                    device_id_type=pl.DeviceIdType.MESH,
                )

    list_copies = []
    lists = ((rows_hbm, rows_list), (nodes_hbm, nodes_list), (counts_hbm, counts), (weights_hbm, weights))
    for i, (source, target) in enumerate(lists):
        list_copies.append(pltpu.make_async_copy(source, target, list_sem.at[i]))
        list_copies[-1].start()
    stripes = panel_sem.shape[0] - 1
    stripe = depth // stripes
    panel_copies = []
    for p in range(stripes):
        where = pl.ds(p * stripe, stripe)
        panel_copies.append(
            pltpu.make_async_copy(panels.at[0, where], shapes.at[where], panel_sem.at[p])
        )
        panel_copies[-1].start()

    def piece_of(index):
        q, h = divmod(index, parts)
        return q, pl.ds(h * span, span)

    def aic_piece(index, peer):
        q, h = divmod(index, parts)
        start = pl.multiple_of(peer * depth + h * span, 128)
        return aic.at[pl.ds(q * sub, sub), pl.ds(start, span)]

    for index in range(total_pieces):
        q, where = piece_of(index)
        pltpu.make_async_copy(
            aic_piece(index, b), influence.at[q, b, :, where], aic_recv.at[index]
        ).start()
    half = cols // 2
    share = dofs // 2
    dof_span = pl.ds((c // half) * share, share)
    sends_modes = lax.rem(c, half) == 0
    own_modes = pltpu.make_async_copy(
        node_modes.at[dof_span], mode_rows.at[dof_span, b], panel_sem.at[stripes]
    )

    @pl.when(sends_modes)
    def _():
        own_modes.start()

    pl.semaphore_wait(barrier, blocks + cols - 2)

    def send_piece(index, parity):
        if index >= total_pieces:
            return
        q, where = piece_of(index)

        @pl.when(lax.rem(c, 2) == parity)
        def _():
            for j in range(blocks - 1):
                peer = far_target(j)
                remote(
                    {"blk": peer},
                    aic_piece(index, peer),
                    influence.at[q, b, :, where],
                    aic_send,
                    aic_recv.at[index],
                ).start()

    def await_piece(index):
        q, where = piece_of(index)
        settle(influence.at[q, :, :, where], aic_recv.at[index])
        send_piece(index + AHEAD, 0)
        send_piece(index + ODD_AHEAD, 1)

    for index in range(max(AHEAD, ODD_AHEAD)):
        if index < AHEAD:
            send_piece(index, 0)
        if index < ODD_AHEAD:
            send_piece(index, 1)

    row_at = lax.broadcasted_iota(jnp.int32, (sub, length), 0)
    column_at = lax.broadcasted_iota(jnp.int32, (sub, length), 1)
    total = jnp.zeros((sub, length), jnp.float32)
    for copy in list_copies:
        copy.wait()
    for o in range(owners):
        for s in range(slots):
            live = s < counts[0, 0, o]
            row = jnp.where(live, rows_list[0, 0, o, s], -1)
            node = nodes_list[0, 0, o, s] + o * node_count
            spread = jnp.zeros((sub, length), jnp.float32)
            for d in range(dofs):
                spread = jnp.where(
                    column_at == node + d * owners * node_count,
                    weights[0, 0, d, o, s],
                    spread,
                )
            total = total + jnp.where(row_at == row, spread, 0.0)
    spline[c, b] = total

    for p in range(stripes):
        panel_copies[p].wait()
        where = pl.ds(p * stripe, stripe)
        high, low = split(shapes[where])
        shapes_high[where] = high
        shapes_low[where] = low

    def multiply(q, start, stop):
        where = pl.ds(start * span, (stop - start) * span)
        lines = blocks * sub
        high, low = split(influence[q, :, :, where].reshape(lines, (stop - start) * span))
        product = jnp.dot(
            jnp.concatenate([high, low], axis=0),
            shapes_high[where],
            preferred_element_type=jnp.float32,
        )
        rest = jnp.dot(high, shapes_low[where], preferred_element_type=jnp.float32)
        return product[:lines] + (product[lines:] + rest)

    def to_plane(q):
        partial[q] = multiply(q, 0, parts).reshape(blocks, sub, width)
        for k in range(1, cols):
            remote(
                {"col": on_plane(k)},
                partial.at[q, on_plane(k)],
                plane_in.at[q, k - 1],
                plane_send,
                plane_recv.at[q],
            ).start()

    def keeper(q):
        return middle - 1 + q % 2 if q in OWNED else None

    def over_plane(q):
        settle(plane_in.at[q], plane_recv.at[q])
        total = partial[q, c]
        for k in range(1, cols):
            total = total + plane_in[q, k - 1]
        line_in[q, b] = total
        keep = keeper(q)
        if keep is None:
            for j in range(blocks - 1):
                remote(
                    {"blk": far_target(j)},
                    line_in.at[q, b],
                    line_in.at[q, b],
                    line_send.at[q],
                    line_recv.at[q],
                ).start()
        else:

            @pl.when(b != keep)
            def _():
                remote(
                    {"blk": keep},
                    line_in.at[q, b],
                    line_in.at[q, b],
                    line_send.at[q],
                    line_recv.at[q],
                ).start()

    def sum_line(q):
        settle(line_in.at[q, pl.ds(0, blocks - 1)], line_recv.at[q])
        total = line_in[q, 0]
        for source in range(1, blocks):
            total = total + line_in[q, source]
        pressure[q, c] = total

    def to_final(q):
        for k in range(1, cols):
            remote(
                {"col": on_plane(k)},
                pressure.at[q, c],
                pressure.at[q, c],
                final_send,
                final_recv.at[q],
            ).start()

    def keep_line(q):
        keep = keeper(q)
        if keep is None:
            return

        @pl.when(b == keep)
        def _():
            sum_line(q)
            for j in range(blocks - 1):
                remote(
                    {"blk": far_target(j)},
                    pressure.at[q, c],
                    pressure.at[q, c],
                    line_send.at[q],
                    back_recv.at[q],
                ).start()
            to_final(q)

    def finish_line(q):
        keep = keeper(q)
        if keep is None:
            sum_line(q)
            to_final(q)
        else:

            @pl.when(b != keep)
            def _():
                settle(pressure.at[q, c], back_recv.at[q])
                to_final(q)

    def seat(r):
        return middle - 1 + r % 2

    is_owner = b == middle - 1 + lax.rem(c, 2)

    def to_owners():
        for r in range(cols):

            @pl.when(jnp.logical_or(b != seat(r), c != r))
            def _():
                remote(
                    {"blk": seat(r), "col": r},
                    partial.at[last, r],
                    gather_in.at[b * cols + c],
                    gather_send,
                    gather_recv,
                ).start()

    def cast():
        @pl.when(is_owner)
        def _():
            gather_in[b * cols + c] = partial[last, c]
            settle(gather_in.at[pl.ds(0, blocks * cols - 1)], gather_recv)
            total = gather_in[0]
            for source in range(1, blocks * cols):
                total = total + gather_in[source]
            pressure[last, c] = total
            for j in range(blocks):
                for k in range(cols):
                    if j == blocks - 1 and k == 0:
                        continue
                    peer = b if j == blocks - 1 else far_target(j)
                    remote(
                        {"blk": peer, "col": on_plane(k)},
                        pressure.at[last, c],
                        pressure.at[last, c],
                        cast_send,
                        cast_recv,
                    ).start()

    def await_cast():
        @pl.when(is_owner)
        def _():
            settle(pressure.at[last, pl.ds(0, cols - 1)], cast_recv)

        @pl.when(jnp.logical_not(is_owner))
        def _():
            settle(pressure.at[last], cast_recv)

    def spline_to_line():
        for j in range(blocks - 1):
            remote(
                {"blk": far_target(j)},
                spline.at[c, b],
                spline.at[c, b],
                spline_send.at[0],
                spline_recv.at[0],
            ).start()

        @pl.when(sends_modes)
        def _():
            for j in range(blocks - 1):
                remote(
                    {"blk": far_target(j)},
                    node_modes.at[dof_span],
                    mode_rows.at[dof_span, b],
                    mode_send.at[0],
                    mode_recv,
                ).start()

    def spline_to_plane():
        settle(spline.at[c, pl.ds(0, blocks - 1)], spline_recv.at[0])
        for k in range(1, cols):
            remote(
                {"col": on_plane(k)},
                spline.at[c],
                spline.at[c],
                spline_send.at[1],
                spline_recv.at[1],
            ).start()

        @pl.when(sends_modes)
        def _():
            own_modes.wait()
            settle(mode_rows.at[dof_span, pl.ds(0, blocks - 1)], mode_recv)
            for k in range(1, cols):
                remote(
                    {"col": on_plane(k)},
                    mode_rows.at[dof_span],
                    mode_rows.at[dof_span],
                    mode_send.at[k],
                    mode_plane_recv.at[c // half],
                ).start()

    def make_force():
        settle(spline.at[pl.ds(0, cols - 1)], spline_recv.at[1])
        for s in range(2):

            @pl.when(c != s * half)
            def _():
                settle(mode_rows.at[pl.ds(s * share, share)], mode_plane_recv.at[s])

        force[...] = jnp.dot(
            spline[...].reshape(cols * blocks * sub, length),
            mode_rows[...].reshape(length, modes),
            precision=HIGHEST,
            preferred_element_type=jnp.float32,
        )

    def modal(start, stop):
        force_rows = force[pl.ds(start * blocks * sub, (stop - start) * blocks * sub)]
        return lax.dot_general(
            force_rows,
            pressure[start:stop].reshape((stop - start) * blocks * sub, width),
            (((0,), (0,)), ((), ())),
            precision=HIGHEST,
            preferred_element_type=jnp.float32,
        )

    for index in range(total_pieces):
        await_piece(index)
        if index == LISTS_AT:
            spline_to_line()
        q, h = divmod(index, parts)
        if q == last:
            product = multiply(last, h, h + 1)
            ending = product if h == 0 else ending + product
            if h == 0:
                keep_line(0)
        elif h == parts - 1:
            to_plane(q)
            if q > 0:
                over_plane(q - 1)
        if index == SPREAD_AT and index < total_pieces - 1:
            spline_to_plane()
    partial[last] = ending.reshape(blocks, sub, width)
    to_owners()
    if SPREAD_AT >= total_pieces - 1:
        spline_to_plane()
    over_plane(last - 1)
    finish_line(0)
    cast()
    for q in range(1, last):
        finish_line(q)
    make_force()
    for q in early:
        settle(pressure.at[q, pl.ds(0, cols - 1)], final_recv.at[q])
    out[...] = modal(0, last)
    await_cast()
    out[...] += modal(last, chunks)

    settle(influence.at[pl.ds(0, blocks - 1)], aic_send)
    settle(plane_in, plane_send)
    settle(plane_in, final_send)
    settle(spline.at[c, pl.ds(0, blocks - 1)], spline_send.at[0])
    settle(spline.at[pl.ds(0, cols - 1)], spline_send.at[1])
    for q in early:
        keep = keeper(q)
        if keep is None:
            settle(line_in.at[q, pl.ds(0, blocks - 1)], line_send.at[q])
        else:

            @pl.when(b == keep)
            def _():
                settle(line_in.at[q, pl.ds(0, blocks - 1)], line_send.at[q])

            @pl.when(b != keep)
            def _():
                settle(line_in.at[q, 0], line_send.at[q])

    @pl.when(is_owner)
    def _():
        settle(partial.at[last, pl.ds(0, cols - 1)], gather_send)
        settle(gather_in.at[pl.ds(0, blocks * cols - 1)], cast_send)

    @pl.when(jnp.logical_not(is_owner))
    def _():
        settle(partial.at[last], gather_send)

    @pl.when(sends_modes)
    def _():
        settle(mode_rows.at[dof_span, pl.ds(0, blocks - 1)], mode_send.at[0])
        settle(mode_rows.at[dof_span], mode_send.at[1])
        for k in range(2, cols):
            settle(mode_rows.at[dof_span], mode_send.at[k])


def by_kernel(aic, downwash, node_modes, src_rows, dst_nodes, counts, spline_weights):
    blocks = lax.axis_size("blk")
    cols = lax.axis_size("col")
    rows = aic.shape[0]
    sub = rows // cols
    depth, width = downwash.shape[1:]
    dofs, node_count, modes = node_modes.shape
    length = dofs * blocks * node_count
    stripes = 4
    dma = pltpu.SemaphoreType.DMA
    anywhere = pl.BlockSpec(memory_space=pl.ANY)
    operands = (aic, downwash, node_modes, src_rows, dst_nodes, counts, spline_weights)
    in_hbm = [pltpu.with_memory_space_constraint(v, pltpu.MemorySpace.HBM) for v in operands]
    return pl.pallas_call(
        functools.partial(exchange_kernel, blocks, cols),
        name="gaf_exchange",
        out_shape=jax.ShapeDtypeStruct((modes, width), jnp.float32),
        in_specs=[anywhere] * 7,
        out_specs=pl.BlockSpec(memory_space=pltpu.VMEM),
        scratch_shapes=[
            pltpu.VMEM((cols, blocks, sub, depth), jnp.float32),
            pltpu.VMEM((depth, width), jnp.float32),
            pltpu.VMEM((depth, width), jnp.bfloat16),
            pltpu.VMEM((depth, width), jnp.bfloat16),
            pltpu.VMEM((cols, blocks, sub, width), jnp.float32),
            pltpu.VMEM((cols - 1, cols - 1, sub, width), jnp.float32),
            pltpu.VMEM((cols - 1, blocks, sub, width), jnp.float32),
            pltpu.VMEM((blocks * cols, sub, width), jnp.float32),
            pltpu.VMEM((cols, blocks, sub, width), jnp.float32),
            pltpu.VMEM((cols, blocks, sub, length), jnp.float32),
            pltpu.VMEM((dofs, blocks, node_count, modes), jnp.float32),
            pltpu.VMEM((cols * blocks * sub, modes), jnp.float32),
            pltpu.SMEM(src_rows.shape, jnp.int32),
            pltpu.SMEM(dst_nodes.shape, jnp.int32),
            pltpu.SMEM(counts.shape, jnp.int32),
            pltpu.SMEM(spline_weights.shape, jnp.float32),
            dma((4,)),
            dma((stripes + 1,)),
            dma((cols * PARTS,)),
            dma,
            dma((cols - 1,)),
            dma,
            dma((cols - 1,)),
            dma((cols - 1,)),
            dma((cols - 1,)),
            dma((cols - 1,)),
            dma,
            dma,
            dma,
            dma,
            dma,
            dma((2,)),
            dma((2,)),
            dma,
            dma((cols,)),
            dma((2,)),
        ],
        compiler_params=pltpu.CompilerParams(
            collective_id=0, has_side_effects=True, vmem_limit_bytes=32 * 1024 * 1024
        ),
    )(*in_hbm)


def solution(mesh):
    placed = (
        P(("groups", "blk"), "col"),
        P(("groups", "col"), "blk", None),
        P(None, "blk", None),
        P("blk", "col", None, None),
        P("blk", "col", None, None),
        P("blk", "col", None),
        P("blk", "col", None, None, None),
    )

    def shards(*operands):
        aic, downwash, node_modes = operands[:3]
        blocks, cols = lax.axis_size("blk"), lax.axis_size("col")
        small = blocks * aic.shape[0] <= 2 * node_modes.shape[2]
        even = blocks == cols and cols % 2 == 0 and node_modes.shape[0] % 2 == 0 and aic.shape[0] % (8 * cols) == 0 and downwash.shape[1] % 512 == 0
        if small and even:
            return by_kernel(*operands)
        return by_rotation(*operands)

    return jax.shard_map(
        shards, mesh=mesh, in_specs=placed, out_specs=P("groups", None), check_vma=False
    )
```

time: 43.7 us -> 40.9 us (0.936)
  Pallas kernels: 42.8 us -> 40 us
    pallas_call x1, Pallas kernels: 42.8 us -> 40 us  [by_kernel(): pl.pallas_call(functools.partial(exchange_kernel, blocks, cols), name='ga...]
where the time goes in v2:
time: 40.9 us; the launch traced here: 40.7 us
  Pallas kernels  40 us (98%)
  local copies, waits for them, and re-layouts  0.72 us (2%)
    pallas_call x1, Pallas kernels, by_kernel(): pl.pallas_call(functools.partial(exchange_kernel, blocks, cols), name='ga...  40 us

profile of v2, /device:TPU:0, one launch (start us, length us, event | category | flops | bytes accessed | tf_op | source)
XLA Modules:
  0.0 40.7 jit_solution(15521230564946117745)
XLA Ops:
  0.0 40.0 %gaf_exchange.1 = f32[192,384]{1,0:T(8,128)S(1)} custom-call(f32[32,8192]{1,0:T(8,128)} %aic.1, f32[1,2048,384]{2,1,0:T(8,128)} %panels.1, f32[6,8,192]{2,1,0:T(8,128)} %node_modes.1, s32[1,1,4,8]{3,2,1,0:T(4,128)} %rows_hbm.1, s32[1,1,4,8]{3,2,1,0:T(4,128)} %nodes_hbm.1, s32[1,1,4]{2,1,0:T(1,128)} %counts_hbm.1, f32[1,1,6,4,8]{4,3,2,1,0:T(4,128)} %weights_hbm.1), custom_call_target="tpu_custom_call" | custom-call | tf_op jit(solution)/shard_map/gaf_exchange/pallas_call | solution.py:595
  40.0 0.7 %copy.9 = f32[192,384]{1,0:T(8,128)} copy(f32[192,384]{1,0:T(8,128)S(1)} %gaf_exchange.1) | data formatting | bytes 589824

commit v3 on v2

--- a/solution.py
+++ b/solution.py
@@ -10,10 +10,14 @@
 
 HIGHEST = lax.Precision.HIGHEST
 PARTS = 2
-AHEAD = 4
-OWNED = (0,)
-LISTS_AT = 3
-SPREAD_AT = 7
+AHEAD = 3
+SECOND_AT = 1
+THIRD_AT = 4
+OPENING = 2
+LAST_AT = None
+AFTER = {4: ((0, 0),), 6: ((0, 1),)}
+TAIL = ((0, 2), (1, 0), (1, 1), (1, 2))
+FINAL = ()
 ODD_AHEAD = 2
 
 
@@ -109,8 +113,9 @@
     shapes_high,
     shapes_low,
     partial,
-    plane_in,
-    line_in,
+    half_in,
+    half_out,
+    cross_in,
     gather_in,
     pressure,
     spline,
@@ -124,17 +129,18 @@
     panel_sem,
     aic_recv,
     aic_send,
-    plane_recv,
-    plane_send,
-    line_recv,
-    line_send,
-    back_recv,
+    half_recv,
+    half_send,
+    cross_recv,
+    cross_send,
     final_recv,
     final_send,
     gather_recv,
     gather_send,
     cast_recv,
     cast_send,
+    chain_recv,
+    chain_send,
     spline_recv,
     spline_send,
     mode_recv,
@@ -224,7 +230,7 @@
     half = cols // 2
     share = dofs // 2
     dof_span = pl.ds((c // half) * share, share)
-    sends_modes = lax.rem(c, half) == 0
+    sends_modes = lax.rem(c, half) == half - 1
     own_modes = pltpu.make_async_copy(
         node_modes.at[dof_span], mode_rows.at[dof_span, b], panel_sem.at[stripes]
     )
@@ -258,11 +264,110 @@
         send_piece(index + AHEAD, 0)
         send_piece(index + ODD_AHEAD, 1)
 
-    for index in range(max(AHEAD, ODD_AHEAD)):
-        if index < AHEAD:
-            send_piece(index, 0)
-        if index < ODD_AHEAD:
-            send_piece(index, 1)
+    own = jnp.where(b < middle, 0, middle)
+    own_pair = pl.ds(own, middle)
+    other_pair = pl.ds(middle - own, middle)
+    near = 2 * own + 1 - b
+    inward = jnp.where(b < middle, middle - 1, middle)
+    team = middle * cols
+    place = (b - own) * cols + c
+    across = blocks - 1 - b
+    inner = jnp.logical_and(b >= middle - 1, b <= middle)
+
+    def chain(stage, peer, blocks_of):
+        remote(
+            {"blk": peer},
+            spline.at[c, blocks_of],
+            spline.at[c, blocks_of],
+            chain_send.at[stage],
+            chain_recv.at[stage],
+        ).start()
+
+    def mode_chain(stage, peer, blocks_of):
+        remote(
+            {"blk": peer},
+            mode_rows.at[dof_span, blocks_of],
+            mode_rows.at[dof_span, blocks_of],
+            mode_send.at[stage],
+            mode_recv.at[stage],
+        ).start()
+
+    def await_chain(stage, count):
+        settle(spline.at[c, pl.ds(0, count)], chain_recv.at[stage])
+
+        @pl.when(sends_modes)
+        def _():
+            settle(mode_rows.at[dof_span, pl.ds(0, count)], mode_recv.at[stage])
+
+    def first_stage_modes():
+        @pl.when(sends_modes)
+        def _():
+            remote(
+                {"blk": near},
+                node_modes.at[dof_span],
+                mode_rows.at[dof_span, b],
+                mode_send.at[0],
+                mode_recv.at[0],
+            ).start()
+
+    def second_stage():
+        await_chain(0, 1)
+
+        @pl.when(sends_modes)
+        def _():
+            own_modes.wait()
+
+        @pl.when(inner)
+        def _():
+            chain(1, across, own_pair)
+
+            @pl.when(sends_modes)
+            def _():
+                mode_chain(1, across, own_pair)
+
+    def third_stage():
+        @pl.when(inner)
+        def _():
+            await_chain(1, middle)
+            chain(2, near, other_pair)
+
+            @pl.when(sends_modes)
+            def _():
+                mode_chain(2, near, other_pair)
+
+            share_lists()
+
+    def last_stage():
+        @pl.when(jnp.logical_not(inner))
+        def _():
+            await_chain(2, middle)
+            share_lists()
+
+    def share_lists():
+        for k in range(1, cols):
+            remote(
+                {"col": on_plane(k)},
+                spline.at[c],
+                spline.at[c],
+                spline_send,
+                spline_recv,
+            ).start()
+
+        @pl.when(sends_modes)
+        def _():
+            for k in range(1, cols):
+                remote(
+                    {"col": on_plane(k)},
+                    mode_rows.at[dof_span],
+                    mode_rows.at[dof_span],
+                    mode_send.at[2 + k],
+                    mode_plane_recv.at[c // half],
+                ).start()
+
+    first_stage_modes()
+    for index in range(OPENING):
+        send_piece(index, 0)
+        send_piece(index, 1)
 
     row_at = lax.broadcasted_iota(jnp.int32, (sub, length), 0)
     column_at = lax.broadcasted_iota(jnp.int32, (sub, length), 1)
@@ -283,6 +388,14 @@
                 )
             total = total + jnp.where(row_at == row, spread, 0.0)
     spline[c, b] = total
+    remote(
+        {"blk": near}, spline.at[c, b], spline.at[c, b], chain_send.at[0], chain_recv.at[0]
+    ).start()
+    for index in range(OPENING, max(AHEAD, ODD_AHEAD)):
+        if index < AHEAD:
+            send_piece(index, 0)
+        if index < ODD_AHEAD:
+            send_piece(index, 1)
 
     for p in range(stripes):
         panel_copies[p].wait()
@@ -303,94 +416,61 @@
         rest = jnp.dot(high, shapes_low[where], preferred_element_type=jnp.float32)
         return product[:lines] + (product[lines:] + rest)
 
-    def to_plane(q):
+    def to_half(q):
         partial[q] = multiply(q, 0, parts).reshape(blocks, sub, width)
-        for k in range(1, cols):
-            remote(
-                {"col": on_plane(k)},
-                partial.at[q, on_plane(k)],
-                plane_in.at[q, k - 1],
-                plane_send,
-                plane_recv.at[q],
-            ).start()
-
-    def keeper(q):
-        return middle - 1 + q % 2 if q in OWNED else None
-
-    def over_plane(q):
-        settle(plane_in.at[q], plane_recv.at[q])
-        total = partial[q, c]
-        for k in range(1, cols):
-            total = total + plane_in[q, k - 1]
-        line_in[q, b] = total
-        keep = keeper(q)
-        if keep is None:
-            for j in range(blocks - 1):
-                remote(
-                    {"blk": far_target(j)},
-                    line_in.at[q, b],
-                    line_in.at[q, b],
-                    line_send.at[q],
-                    line_recv.at[q],
-                ).start()
-        else:
-
-            @pl.when(b != keep)
+        for r in range(cols):
+
+            @pl.when(jnp.logical_or(b != inward, c != r))
             def _():
                 remote(
-                    {"blk": keep},
-                    line_in.at[q, b],
-                    line_in.at[q, b],
-                    line_send.at[q],
-                    line_recv.at[q],
+                    {"blk": inward, "col": r},
+                    partial.at[q, r],
+                    half_in.at[q, place],
+                    half_send,
+                    half_recv.at[q],
                 ).start()
 
-    def sum_line(q):
-        settle(line_in.at[q, pl.ds(0, blocks - 1)], line_recv.at[q])
-        total = line_in[q, 0]
-        for source in range(1, blocks):
-            total = total + line_in[q, source]
-        pressure[q, c] = total
-
-    def to_final(q):
-        for k in range(1, cols):
+        @pl.when(inner)
+        def _():
+            half_in[q, place] = partial[q, c]
+
+    def half_sum(q):
+        @pl.when(inner)
+        def _():
+            settle(half_in.at[q, pl.ds(0, team - 1)], half_recv.at[q])
+            total = half_in[q, 0]
+            for source in range(1, team):
+                total = total + half_in[q, source]
+            half_out[q] = total
             remote(
-                {"col": on_plane(k)},
-                pressure.at[q, c],
-                pressure.at[q, c],
-                final_send,
-                final_recv.at[q],
+                {"blk": across}, half_out.at[q], cross_in.at[q], cross_send, cross_recv.at[q]
             ).start()
 
-    def keep_line(q):
-        keep = keeper(q)
-        if keep is None:
-            return
-
-        @pl.when(b == keep)
-        def _():
-            sum_line(q)
-            for j in range(blocks - 1):
-                remote(
-                    {"blk": far_target(j)},
-                    pressure.at[q, c],
-                    pressure.at[q, c],
-                    line_send.at[q],
-                    back_recv.at[q],
-                ).start()
-            to_final(q)
-
-    def finish_line(q):
-        keep = keeper(q)
-        if keep is None:
-            sum_line(q)
-            to_final(q)
-        else:
-
-            @pl.when(b != keep)
-            def _():
-                settle(pressure.at[q, c], back_recv.at[q])
-                to_final(q)
+    def full_sum(q):
+        @pl.when(inner)
+        def _():
+            settle(cross_in.at[q], cross_recv.at[q])
+            pressure[q, c] = half_out[q] + cross_in[q]
+            for peer in (near, b):
+                for k in range(cols):
+                    if peer is b and k == 0:
+                        continue
+                    remote(
+                        {"blk": peer, "col": on_plane(k)},
+                        pressure.at[q, c],
+                        pressure.at[q, c],
+                        final_send,
+                        final_recv.at[q],
+                    ).start()
+
+    def await_final(q):
+        @pl.when(inner)
+        def _():
+            settle(pressure.at[q, pl.ds(0, cols - 1)], final_recv.at[q])
+
+        @pl.when(jnp.logical_not(inner))
+        def _():
+            settle(pressure.at[q], final_recv.at[q])
 
     def seat(r):
         return middle - 1 + r % 2
@@ -441,56 +521,11 @@
         def _():
             settle(pressure.at[last], cast_recv)
 
-    def spline_to_line():
-        for j in range(blocks - 1):
-            remote(
-                {"blk": far_target(j)},
-                spline.at[c, b],
-                spline.at[c, b],
-                spline_send.at[0],
-                spline_recv.at[0],
-            ).start()
-
-        @pl.when(sends_modes)
-        def _():
-            for j in range(blocks - 1):
-                remote(
-                    {"blk": far_target(j)},
-                    node_modes.at[dof_span],
-                    mode_rows.at[dof_span, b],
-                    mode_send.at[0],
-                    mode_recv,
-                ).start()
-
-    def spline_to_plane():
-        settle(spline.at[c, pl.ds(0, blocks - 1)], spline_recv.at[0])
-        for k in range(1, cols):
-            remote(
-                {"col": on_plane(k)},
-                spline.at[c],
-                spline.at[c],
-                spline_send.at[1],
-                spline_recv.at[1],
-            ).start()
-
-        @pl.when(sends_modes)
-        def _():
-            own_modes.wait()
-            settle(mode_rows.at[dof_span, pl.ds(0, blocks - 1)], mode_recv)
-            for k in range(1, cols):
-                remote(
-                    {"col": on_plane(k)},
-                    mode_rows.at[dof_span],
-                    mode_rows.at[dof_span],
-                    mode_send.at[k],
-                    mode_plane_recv.at[c // half],
-                ).start()
-
     def make_force():
-        settle(spline.at[pl.ds(0, cols - 1)], spline_recv.at[1])
+        settle(spline.at[pl.ds(0, cols - 1)], spline_recv)
         for s in range(2):
 
-            @pl.when(c != s * half)
+            @pl.when(c != s * half + half - 1)
             def _():
                 settle(mode_rows.at[pl.ds(s * share, share)], mode_plane_recv.at[s])
 
@@ -502,65 +537,66 @@
         )
 
     def modal(start, stop):
-        force_rows = force[pl.ds(start * blocks * sub, (stop - start) * blocks * sub)]
+        rows = (stop - start) * blocks * sub
+        force_high, force_low = split(force[pl.ds(start * blocks * sub, rows)])
+        high, low = split(pressure[start:stop].reshape(rows, width))
         return lax.dot_general(
-            force_rows,
-            pressure[start:stop].reshape((stop - start) * blocks * sub, width),
+            jnp.concatenate([force_high, force_high, force_low], axis=0),
+            jnp.concatenate([high, low, high], axis=0),
             (((0,), (0,)), ((), ())),
-            precision=HIGHEST,
             preferred_element_type=jnp.float32,
         )
 
     for index in range(total_pieces):
         await_piece(index)
-        if index == LISTS_AT:
-            spline_to_line()
         q, h = divmod(index, parts)
         if q == last:
             product = multiply(last, h, h + 1)
             ending = product if h == 0 else ending + product
-            if h == 0:
-                keep_line(0)
         elif h == parts - 1:
-            to_plane(q)
-            if q > 0:
-                over_plane(q - 1)
-        if index == SPREAD_AT and index < total_pieces - 1:
-            spline_to_plane()
+            to_half(q)
+        if index == SECOND_AT:
+            second_stage()
+        if index == THIRD_AT:
+            third_stage()
+        if index == LAST_AT:
+            last_stage()
+        for kind, q in AFTER.get(index, ()):
+            (half_sum, full_sum)[kind](q)
     partial[last] = ending.reshape(blocks, sub, width)
     to_owners()
-    if SPREAD_AT >= total_pieces - 1:
-        spline_to_plane()
-    over_plane(last - 1)
-    finish_line(0)
+    if LAST_AT is None:
+        last_stage()
+    for kind, q in TAIL:
+        (half_sum, full_sum)[kind](q)
     cast()
-    for q in range(1, last):
-        finish_line(q)
+    for kind, q in FINAL:
+        (half_sum, full_sum)[kind](q)
     make_force()
     for q in early:
-        settle(pressure.at[q, pl.ds(0, cols - 1)], final_recv.at[q])
+        await_final(q)
     out[...] = modal(0, last)
     await_cast()
     out[...] += modal(last, chunks)
 
     settle(influence.at[pl.ds(0, blocks - 1)], aic_send)
-    settle(plane_in, plane_send)
-    settle(plane_in, final_send)
-    settle(spline.at[c, pl.ds(0, blocks - 1)], spline_send.at[0])
-    settle(spline.at[pl.ds(0, cols - 1)], spline_send.at[1])
-    for q in early:
-        keep = keeper(q)
-        if keep is None:
-            settle(line_in.at[q, pl.ds(0, blocks - 1)], line_send.at[q])
-        else:
-
-            @pl.when(b == keep)
-            def _():
-                settle(line_in.at[q, pl.ds(0, blocks - 1)], line_send.at[q])
-
-            @pl.when(b != keep)
-            def _():
-                settle(line_in.at[q, 0], line_send.at[q])
+    settle(spline.at[c, 0], chain_send.at[0])
+
+    @pl.when(inner)
+    def _():
+        settle(spline.at[c, pl.ds(0, middle)], chain_send.at[1])
+        settle(spline.at[c, pl.ds(0, middle)], chain_send.at[2])
+
+    settle(spline.at[pl.ds(0, cols - 1)], spline_send)
+    @pl.when(inner)
+    def _():
+        settle(partial.at[pl.ds(0, last), pl.ds(0, cols - 1)], half_send)
+        settle(half_out, cross_send)
+        settle(half_in.at[:, pl.ds(0, team - 1)], final_send)
+
+    @pl.when(jnp.logical_not(inner))
+    def _():
+        settle(partial.at[pl.ds(0, last)], half_send)
 
     @pl.when(is_owner)
     def _():
@@ -573,10 +609,15 @@
 
     @pl.when(sends_modes)
     def _():
-        settle(mode_rows.at[dof_span, pl.ds(0, blocks - 1)], mode_send.at[0])
-        settle(mode_rows.at[dof_span], mode_send.at[1])
-        for k in range(2, cols):
-            settle(mode_rows.at[dof_span], mode_send.at[k])
+        settle(mode_rows.at[dof_span, 0], mode_send.at[0])
+
+        @pl.when(inner)
+        def _():
+            settle(mode_rows.at[dof_span, pl.ds(0, middle)], mode_send.at[1])
+            settle(mode_rows.at[dof_span, pl.ds(0, middle)], mode_send.at[2])
+
+        for k in range(1, cols):
+            settle(mode_rows.at[dof_span], mode_send.at[2 + k])
 
 
 def by_kernel(aic, downwash, node_modes, src_rows, dst_nodes, counts, spline_weights):
@@ -604,8 +645,9 @@
             pltpu.VMEM((depth, width), jnp.bfloat16),
             pltpu.VMEM((depth, width), jnp.bfloat16),
             pltpu.VMEM((cols, blocks, sub, width), jnp.float32),
-            pltpu.VMEM((cols - 1, cols - 1, sub, width), jnp.float32),
-            pltpu.VMEM((cols - 1, blocks, sub, width), jnp.float32),
+            pltpu.VMEM((cols - 1, blocks // 2 * cols, sub, width), jnp.float32),
+            pltpu.VMEM((cols - 1, sub, width), jnp.float32),
+            pltpu.VMEM((cols - 1, sub, width), jnp.float32),
             pltpu.VMEM((blocks * cols, sub, width), jnp.float32),
             pltpu.VMEM((cols, blocks, sub, width), jnp.float32),
             pltpu.VMEM((cols, blocks, sub, length), jnp.float32),
@@ -622,18 +664,19 @@
             dma((cols - 1,)),
             dma,
             dma((cols - 1,)),
+            dma,
             dma((cols - 1,)),
-            dma((cols - 1,)),
-            dma((cols - 1,)),
-            dma,
-            dma,
-            dma,
-            dma,
-            dma,
-            dma((2,)),
-            dma((2,)),
-            dma,
-            dma((cols,)),
+            dma,
+            dma,
+            dma,
+            dma,
+            dma,
+            dma((3,)),
+            dma((3,)),
+            dma,
+            dma,
+            dma((3,)),
+            dma((2 + cols,)),
             dma((2,)),
         ],
         compiler_params=pltpu.CompilerParams(
@@ -657,7 +700,7 @@
         aic, downwash, node_modes = operands[:3]
         blocks, cols = lax.axis_size("blk"), lax.axis_size("col")
         small = blocks * aic.shape[0] <= 2 * node_modes.shape[2]
-        even = blocks == cols and cols % 2 == 0 and node_modes.shape[0] % 2 == 0 and aic.shape[0] % (8 * cols) == 0 and downwash.shape[1] % 512 == 0
+        even = blocks == cols == 4 and cols % 2 == 0 and node_modes.shape[0] % 2 == 0 and aic.shape[0] % (8 * cols) == 0 and downwash.shape[1] % 512 == 0
         if small and even:
             return by_kernel(*operands)
         return by_rotation(*operands)

time: 40.9 us -> 39.5 us (0.966)
  Pallas kernels: 40 us -> 38.6 us
    pallas_call x1, Pallas kernels: 40 us -> 38.6 us  [by_kernel(): pl.pallas_call(functools.partial(exchange_kernel, blocks, cols), name='ga...]
where the time goes in v3:
time: 39.5 us; the launch traced here: 39.4 us
  Pallas kernels  38.6 us (98%)
  local copies, waits for them, and re-layouts  0.72 us (2%)
    pallas_call x1, Pallas kernels, by_kernel(): pl.pallas_call(functools.partial(exchange_kernel, blocks, cols), name='ga...  38.6 us

profile of v3, /device:TPU:0, one launch (start us, length us, event | category | flops | bytes accessed | tf_op | source)
XLA Modules:
  0.0 39.4 jit_solution(11777049780545937843)
XLA Ops:
  0.0 38.6 %gaf_exchange.1 = f32[192,384]{1,0:T(8,128)S(1)} custom-call(f32[32,8192]{1,0:T(8,128)} %aic.1, f32[1,2048,384]{2,1,0:T(8,128)} %panels.1, f32[6,8,192]{2,1,0:T(8,128)} %node_modes.1, s32[1,1,4,8]{3,2,1,0:T(4,128)} %rows_hbm.1, s32[1,1,4,8]{3,2,1,0:T(4,128)} %nodes_hbm.1, s32[1,1,4]{2,1,0:T(1,128)} %counts_hbm.1, f32[1,1,6,4,8]{4,3,2,1,0:T(4,128)} %weights_hbm.1), custom_call_target="tpu_custom_call" | custom-call | tf_op jit(solution)/shard_map/gaf_exchange/pallas_call | solution.py:636
  38.6 0.7 %copy.9 = f32[192,384]{1,0:T(8,128)} copy(f32[192,384]{1,0:T(8,128)S(1)} %gaf_exchange.1) | data formatting | bytes 589824

commit v4 on v3

--- a/solution.py
+++ b/solution.py
@@ -14,9 +14,10 @@
 SECOND_AT = 1
 THIRD_AT = 4
 OPENING = 2
-LAST_AT = None
+LAST_AT = 6
+LATE_FROM = 2
 AFTER = {4: ((0, 0),), 6: ((0, 1),)}
-TAIL = ((0, 2), (1, 0), (1, 1), (1, 2))
+TAIL = ((1, 0), (1, 1), (1, 2))
 FINAL = ()
 ODD_AHEAD = 2
 
@@ -564,20 +565,23 @@
         for kind, q in AFTER.get(index, ()):
             (half_sum, full_sum)[kind](q)
     partial[last] = ending.reshape(blocks, sub, width)
-    to_owners()
     if LAST_AT is None:
         last_stage()
+    half_sum(last - 1)
+    to_owners()
     for kind, q in TAIL:
         (half_sum, full_sum)[kind](q)
     cast()
     for kind, q in FINAL:
         (half_sum, full_sum)[kind](q)
     make_force()
-    for q in early:
+    for q in range(LATE_FROM):
         await_final(q)
-    out[...] = modal(0, last)
+    out[...] = modal(0, LATE_FROM)
+    for q in range(LATE_FROM, last):
+        await_final(q)
     await_cast()
-    out[...] += modal(last, chunks)
+    out[...] += modal(LATE_FROM, chunks)
 
     settle(influence.at[pl.ds(0, blocks - 1)], aic_send)
     settle(spline.at[c, 0], chain_send.at[0])

time: 39.5 us -> 39.4 us (level)
  no operation moved by 1% of the time
where the time goes in v4:
time: 39.4 us; the launch traced here: 39.2 us
  Pallas kernels  38.5 us (98%)
  local copies, waits for them, and re-layouts  0.72 us (2%)
    pallas_call x1, Pallas kernels, by_kernel(): pl.pallas_call(functools.partial(exchange_kernel, blocks, cols), name='ga...  38.5 us

profile of v4, /device:TPU:0, one launch (start us, length us, event | category | flops | bytes accessed | tf_op | source)
XLA Modules:
  0.0 39.2 jit_solution(13821767508483205927)
XLA Ops:
  0.0 38.5 %gaf_exchange.1 = f32[192,384]{1,0:T(8,128)S(1)} custom-call(f32[32,8192]{1,0:T(8,128)} %aic.1, f32[1,2048,384]{2,1,0:T(8,128)} %panels.1, f32[6,8,192]{2,1,0:T(8,128)} %node_modes.1, s32[1,1,4,8]{3,2,1,0:T(4,128)} %rows_hbm.1, s32[1,1,4,8]{3,2,1,0:T(4,128)} %nodes_hbm.1, s32[1,1,4]{2,1,0:T(1,128)} %counts_hbm.1, f32[1,1,6,4,8]{4,3,2,1,0:T(4,128)} %weights_hbm.1), custom_call_target="tpu_custom_call" | custom-call | tf_op jit(solution)/shard_map/gaf_exchange/pallas_call | solution.py:640
  38.5 0.7 %copy.9 = f32[192,384]{1,0:T(8,128)} copy(f32[192,384]{1,0:T(8,128)S(1)} %gaf_exchange.1) | data formatting | bytes 589824

commit v5 on v4

--- a/solution.py
+++ b/solution.py
@@ -17,7 +17,7 @@
 LAST_AT = 6
 LATE_FROM = 2
 AFTER = {4: ((0, 0),), 6: ((0, 1),)}
-TAIL = ((1, 0), (1, 1), (1, 2))
+TAIL = ((0, 2), (1, 0), (1, 1), (1, 2))
 FINAL = ()
 ODD_AHEAD = 2
 
@@ -476,15 +476,19 @@
     def seat(r):
         return middle - 1 + r % 2
 
-    is_owner = b == middle - 1 + lax.rem(c, 2)
+    def chair(r):
+        return r // 2 * 2 + 1
+
+    is_owner = jnp.logical_and(inner, lax.rem(c, 2) == 1)
+    mine = jnp.where(inner, c // 2 * 2 + b - (middle - 1), 0)
 
     def to_owners():
         for r in range(cols):
 
-            @pl.when(jnp.logical_or(b != seat(r), c != r))
+            @pl.when(jnp.logical_or(b != seat(r), c != chair(r)))
             def _():
                 remote(
-                    {"blk": seat(r), "col": r},
+                    {"blk": seat(r), "col": chair(r)},
                     partial.at[last, r],
                     gather_in.at[b * cols + c],
                     gather_send,
@@ -494,12 +498,12 @@
     def cast():
         @pl.when(is_owner)
         def _():
-            gather_in[b * cols + c] = partial[last, c]
+            gather_in[b * cols + c] = partial[last, mine]
             settle(gather_in.at[pl.ds(0, blocks * cols - 1)], gather_recv)
             total = gather_in[0]
             for source in range(1, blocks * cols):
                 total = total + gather_in[source]
-            pressure[last, c] = total
+            pressure[last, mine] = total
             for j in range(blocks):
                 for k in range(cols):
                     if j == blocks - 1 and k == 0:
@@ -507,8 +511,8 @@
                     peer = b if j == blocks - 1 else far_target(j)
                     remote(
                         {"blk": peer, "col": on_plane(k)},
-                        pressure.at[last, c],
-                        pressure.at[last, c],
+                        pressure.at[last, mine],
+                        pressure.at[last, mine],
                         cast_send,
                         cast_recv,
                     ).start()
@@ -565,10 +569,9 @@
         for kind, q in AFTER.get(index, ()):
             (half_sum, full_sum)[kind](q)
     partial[last] = ending.reshape(blocks, sub, width)
+    to_owners()
     if LAST_AT is None:
         last_stage()
-    half_sum(last - 1)
-    to_owners()
     for kind, q in TAIL:
         (half_sum, full_sum)[kind](q)
     cast()

time: 39.4 us -> 39.2 us (level)
  no operation moved by 1% of the time
where the time goes in v5:
time: 39.2 us; the launch traced here: 39.1 us
  Pallas kernels  38.4 us (98%)
  local copies, waits for them, and re-layouts  0.72 us (2%)
    pallas_call x1, Pallas kernels, by_kernel(): pl.pallas_call(functools.partial(exchange_kernel, blocks, cols), name='ga...  38.4 us

profile of v5, /device:TPU:0, one launch (start us, length us, event | category | flops | bytes accessed | tf_op | source)
XLA Modules:
  0.0 39.1 jit_solution(2143869707900021621)
XLA Ops:
  0.0 38.4 %gaf_exchange.1 = f32[192,384]{1,0:T(8,128)S(1)} custom-call(f32[32,8192]{1,0:T(8,128)} %aic.1, f32[1,2048,384]{2,1,0:T(8,128)} %panels.1, f32[6,8,192]{2,1,0:T(8,128)} %node_modes.1, s32[1,1,4,8]{3,2,1,0:T(4,128)} %rows_hbm.1, s32[1,1,4,8]{3,2,1,0:T(4,128)} %nodes_hbm.1, s32[1,1,4]{2,1,0:T(1,128)} %counts_hbm.1, f32[1,1,6,4,8]{4,3,2,1,0:T(4,128)} %weights_hbm.1), custom_call_target="tpu_custom_call" | custom-call | tf_op jit(solution)/shard_map/gaf_exchange/pallas_call | solution.py:643
  38.4 0.7 %copy.9 = f32[192,384]{1,0:T(8,128)} copy(f32[192,384]{1,0:T(8,128)S(1)} %gaf_exchange.1) | data formatting | bytes 589824

commit v6 on v5

--- a/solution.py
+++ b/solution.py
@@ -11,8 +11,8 @@
 HIGHEST = lax.Precision.HIGHEST
 PARTS = 2
 AHEAD = 3
-SECOND_AT = 1
-THIRD_AT = 4
+SECOND_AT = 0
+THIRD_AT = 3
 OPENING = 2
 LAST_AT = 6
 LATE_FROM = 2

time: 39.2 us -> 39.1 us (level)
  no operation moved by 1% of the time
where the time goes in v6:
time: 39.1 us; the launch traced here: 39 us
  Pallas kernels  38.3 us (98%)
  local copies, waits for them, and re-layouts  0.72 us (2%)
    pallas_call x1, Pallas kernels, by_kernel(): pl.pallas_call(functools.partial(exchange_kernel, blocks, cols), name='ga...  38.3 us

profile of v6, /device:TPU:0, one launch (start us, length us, event | category | flops | bytes accessed | tf_op | source)
XLA Modules:
  0.0 39.0 jit_solution(16325397960869594855)
XLA Ops:
  0.0 38.3 %gaf_exchange.1 = f32[192,384]{1,0:T(8,128)S(1)} custom-call(f32[32,8192]{1,0:T(8,128)} %aic.1, f32[1,2048,384]{2,1,0:T(8,128)} %panels.1, f32[6,8,192]{2,1,0:T(8,128)} %node_modes.1, s32[1,1,4,8]{3,2,1,0:T(4,128)} %rows_hbm.1, s32[1,1,4,8]{3,2,1,0:T(4,128)} %nodes_hbm.1, s32[1,1,4]{2,1,0:T(1,128)} %counts_hbm.1, f32[1,1,6,4,8]{4,3,2,1,0:T(4,128)} %weights_hbm.1), custom_call_target="tpu_custom_call" | custom-call | tf_op jit(solution)/shard_map/gaf_exchange/pallas_call | solution.py:643
  38.3 0.7 %copy.9 = f32[192,384]{1,0:T(8,128)} copy(f32[192,384]{1,0:T(8,128)S(1)} %gaf_exchange.1) | data formatting | bytes 589824
